TPU v7x, 128 devices: a whole 4x4x4 slice. The times are simulated.
128 devices in a mesh: outer: 8 (over z, core), inner: 16 (over x, y).
Axes of the slice: x: 4, y: 4, z: 4, core: 2. Of those that a mesh axis runs over, the one named last changes fastest.
Arguments:
- queries: bfloat16 [131072, 2048], P(('outer', 'inner')), may hold values from -6 to 6
- key_rows: bfloat16 [131072, 2048], P(('outer', 'inner')), may hold values from -6 to 6
- value_rows: bfloat16 [131072, 2048], P(('outer', 'inner')), may hold values from -6 to 6
- norm_gain: float32 [2048], replicated, may hold values from 0.5 to 1.5
Outputs:
- mixed: bfloat16 [131072, 2048], P(('outer', 'inner'))
- final_state: float32 [131072], P(('outer', 'inner'))
All inputs are finite; a program needn't handle non-finite values.
Results may differ from a plain program's by a relative error of at most 0.005.
Values sent between devices are 32-bit elements; how exact they have to be, the bound alone decides.
No kernel may reach another device: no remote copies, remote signals or barrier semaphores. Data moves between devices by JAX's collectives and lax.ppermute only.
A program may use at most 256 MiB of HBM per device.

v0:
```python
import jax
import jax.numpy as jnp
from jax import lax
from jax.sharding import PartitionSpec as P

D = 2048
HEADS = 32
DK = 64
BLOCK = 128


def carried_in(array, axis, combine, identity):
    length, here = (lax.axis_size(axis), lax.axis_index(axis))
    everything = lax.all_gather(array, axis)
    start = jnp.broadcast_to(jnp.asarray(identity, array.dtype), array.shape)

    def turn(k, before):
        reached = k < here
        new = combine(before, everything[k])
        return jnp.where(reached, new, before)

    return lax.fori_loop(0, length, turn, start)


def from_root(array, axis, root):
    mine = lax.axis_index(axis) == root
    return lax.psum(jnp.where(mine, array, jnp.zeros_like(array)), axis)


def combine_add(earlier, later):
    return earlier + later


def shards(queries, key_rows, value_rows, norm_gain):
    local_rows = queries.shape[0]
    blocks = local_rows // BLOCK
    query_grid = queries.reshape(blocks, BLOCK, HEADS, DK)
    key_grid = key_rows.reshape(blocks, BLOCK, HEADS, DK)
    value_grid = value_rows.reshape(blocks, BLOCK, HEADS, DK)
    block_states = jnp.einsum(
        "nkhd,nkhe->nhde", key_grid, value_grid, preferred_element_type=jnp.float32
    )
    later_index = lax.broadcasted_iota(jnp.int32, (blocks, blocks), 0)
    earlier_index = lax.broadcasted_iota(jnp.int32, (blocks, blocks), 1)
    lower = (earlier_index < later_index).astype(jnp.float32)
    flat_states = block_states.reshape(blocks, HEADS * DK * DK)
    before_block = jnp.dot(
        lower, flat_states, precision=lax.Precision.HIGHEST, preferred_element_type=jnp.float32
    ).reshape(blocks, HEADS, DK, DK)
    own_total = jnp.sum(flat_states, axis=0).reshape(HEADS, DK * DK)
    zero_state = jnp.zeros_like(own_total)
    causal = jnp.tril(jnp.ones((BLOCK, BLOCK), jnp.float32))
    scores = (
        jnp.einsum("nqhd,nkhd->nhqk", query_grid, key_grid, preferred_element_type=jnp.float32)
        * causal
    )
    weights = scores.astype(jnp.bfloat16)
    inside = jnp.einsum("nhqk,nkhe->nqhe", weights, value_grid, preferred_element_type=jnp.float32)
    prefix = carried_in(own_total, ("outer", "inner"), combine_add, zero_state)
    devices = lax.axis_size("outer") * lax.axis_size("inner")
    share = HEADS * DK * DK // devices
    scale_total = float(local_rows * devices) ** (-0.5)
    last_state = from_root(
        (prefix + own_total).reshape(HEADS * DK * DK), ("outer", "inner"), devices - 1
    )
    rank = lax.axis_index("outer") * lax.axis_size("inner") + lax.axis_index("inner")
    own_share = lax.dynamic_slice_in_dim(last_state, rank * share, share, 0)
    final_state = own_share * scale_total
    states = (prefix.reshape(1, HEADS, DK, DK) + before_block).astype(jnp.bfloat16)
    carried = jnp.einsum("nqhd,nhde->nqhe", query_grid, states, preferred_element_type=jnp.float32)
    attended = carried + inside
    gain_grid = norm_gain.reshape(HEADS, DK)
    scaled = (
        attended
        * lax.rsqrt(jnp.mean(attended * attended, axis=-1, keepdims=True) + 1e-06)
        * gain_grid
    )
    mixed = scaled.reshape(local_rows, D).astype(jnp.bfloat16)
    return (mixed, final_state)


def solution(mesh):
    return jax.shard_map(
        shards,
        mesh=mesh,
        in_specs=(
            P(("outer", "inner"), None),
            P(("outer", "inner"), None),
            P(("outer", "inner"), None),
            P(),
        ),
        out_specs=(P(("outer", "inner"), None), P(("outer", "inner"))),
        check_vma=False,
    )
```

profile of v0, /device:TPU:1, one launch (start us, length us, event | category | flops | bytes accessed | tf_op | source)
XLA Modules:
  0.0 548.3 jit_solution(6453652981230500022)
XLA Ops:
  7.2 12.9 %reshape.56 = bf16[8,128,32,64]{3,2,1,0:T(8,128)(2,1)} reshape(bf16[1024,2048]{1,0:T(8,128)(2,1)} %param.7) | data formatting | bytes 8388608 | tf_op jit(solution)/shard_map/reshape | solution.py:38
  20.1 11.5 %copy.35 = bf16[8,128,32,64]{1,3,2,0:T(8,128)(2,1)} copy(bf16[8,128,32,64]{3,2,1,0:T(8,128)(2,1)} %reshape.56) | data formatting | bytes 8388608 | tf_op jit(solution)/shard_map/reshape | solution.py:38
  31.6 12.9 %reshape.57 = bf16[8,128,32,64]{3,2,1,0:T(8,128)(2,1)} reshape(bf16[1024,2048]{1,0:T(8,128)(2,1)} %param.8) | data formatting | bytes 8388608 | tf_op jit(solution)/shard_map/reshape | solution.py:39
  44.4 11.5 %copy.36 = bf16[8,128,32,64]{1,3,2,0:T(8,128)(2,1)} copy(bf16[8,128,32,64]{3,2,1,0:T(8,128)(2,1)} %reshape.57) | data formatting | bytes 8388608 | tf_op jit(solution)/shard_map/reshape | solution.py:39
  55.9 9.0 %fusion.10 = (f32[32,64,64]{2,1,0:T(8,128)S(1)}, f32[8,32,64,64]{3,2,1,0:T(8,128)}) fusion(bf16[8,128,32,64]{1,3,2,0:T(8,128)(2,1)} %copy.35, bf16[8,128,32,64]{1,3,2,0:T(8,128)(2,1)} %copy.36), kind=kOutput, calls=%fused_computation.18 | convolution fusion | flops 269352960 | bytes 13107200 | tf_op jit(solution)/shard_map/nkhd,nkhe->nhde/dot_general | solution.py:40
  66.9 12.9 %reshape.58 = bf16[8,128,32,64]{3,2,1,0:T(8,128)(2,1)} reshape(bf16[1024,2048]{1,0:T(8,128)(2,1)} %param.6) | data formatting | bytes 8388608 | tf_op jit(solution)/shard_map/reshape | solution.py:37
  79.7 11.6 %copy.40 = bf16[8,128,32,64]{1,3,2,0:T(8,128)(2,1)} copy(bf16[8,128,32,64]{3,2,1,0:T(8,128)(2,1)} %reshape.58) | data formatting | bytes 8388608 | tf_op jit(solution)/shard_map/reshape | solution.py:37
  91.3 7.7 %reshape.51 = f32[8,131072]{1,0:T(8,128)} reshape(f32[8,32,64,64]{3,2,1,0:T(8,128)} %get-tuple-element.112) | data formatting | bytes 8388608 | tf_op jit(solution)/shard_map/reshape | solution.py:46
  99.0 8.7 %dot_general.21 = f32[32,64,64,8]{2,1,0,3:T(8,128)} reshape(f32[131072,8]{0,1:T(8,128)} %bitcast.37) | data formatting | bytes 8388608 | tf_op jit(solution)/shard_map/dot_general | solution.py:47
  107.7 126.6 %all-gather.2.cloned.1.call-done = f32[128,32,4096]{2,1,0:T(8,128)} async-done(((f32[1,32,4096]{2,1,0:T(8,128)}), f32[128,32,4096]{2,1,0:T(8,128)}) %all-gather.2.cloned.1.call-update) | async-done | bytes 67108880 | tf_op jit(solution)/shard_map/all_gather | solution.py:14
  234.3 158.9 %while.14 = (s32[]{:T(128)}, f32[32,4096]{1,0:T(8,128)S(1)}, s32[]{:T(128)}, f32[128,32,4096]{2,1,0:T(8,128)}, s32[]{:T(128)}, /*index=5*/s32[]{:T(128)}) while((s32[]{:T(128)}, f32[32,4096]{1,0:T(8,128)S(1)}, s32[]{:T(128)}, f32[128,32,4096]{2,1,0:T(8,128)}, s32[]{:T(128)}, /*index=5*/s32[]{:T(128)}) %tuple.41), condition=%wide.region_2.3_spmd.clone, body=%wide.region_1.2_spmd.clone.sunk | while | flops 393220 | bytes 1572965 | solution.py:22
  235.6 1.2 add_select_fusion.2
  236.8 1.2 add_select_fusion.2
  238.1 1.2 add_select_fusion.2
  239.3 1.2 add_select_fusion.2
  240.5 1.2 add_select_fusion.2
  241.8 1.2 add_select_fusion.2
  243.0 1.2 add_select_fusion.2
  244.3 1.2 add_select_fusion.2
  245.5 1.2 add_select_fusion.2
  246.7 1.2 add_select_fusion.2
  248.0 1.2 add_select_fusion.2
  249.2 1.2 add_select_fusion.2
  250.5 1.2 add_select_fusion.2
  251.7 1.2 add_select_fusion.2
  252.9 1.2 add_select_fusion.2
  254.2 1.2 add_select_fusion.2
  255.4 1.2 add_select_fusion.2
  256.7 1.2 add_select_fusion.2
  257.9 1.2 add_select_fusion.2
  259.1 1.2 add_select_fusion.2
  260.4 1.2 add_select_fusion.2
  261.6 1.2 add_select_fusion.2
  262.9 1.2 add_select_fusion.2
  264.1 1.2 add_select_fusion.2
  265.3 1.2 add_select_fusion.2
  266.6 1.2 add_select_fusion.2
  267.8 1.2 add_select_fusion.2
  269.1 1.2 add_select_fusion.2
  270.3 1.2 add_select_fusion.2
  271.5 1.2 add_select_fusion.2
  272.8 1.2 add_select_fusion.2
  274.0 1.2 add_select_fusion.2
  275.3 1.2 add_select_fusion.2
  276.5 1.2 add_select_fusion.2
  277.7 1.2 add_select_fusion.2
  279.0 1.2 add_select_fusion.2
  280.2 1.2 add_select_fusion.2
  281.5 1.2 add_select_fusion.2
  282.7 1.2 add_select_fusion.2
  283.9 1.2 add_select_fusion.2
  285.2 1.2 add_select_fusion.2
  286.4 1.2 add_select_fusion.2
  287.7 1.2 add_select_fusion.2
  288.9 1.2 add_select_fusion.2
  290.1 1.2 add_select_fusion.2
  394.7 12.6 %add_convert_fusion = bf16[8,32,64,64]{3,0,2,1:T(8,128)(2,1)S(1)} fusion(f32[32,64,64]{2,1,0:T(8,128)S(1)} %add.66, f32[32,64,64,8]{2,1,0,3:T(8,128)} %dot_general.21), kind=kOutput, calls=%fused_computation.7 | convolution fusion | flops 102760512 | bytes 6815744 | tf_op jit(solution)/shard_map/dot_general | solution.py:47
  407.4 4.8 fusion.2
  412.1 14.9 %multiply_reduce_fusion = (f32[8,128,32]{1,2,0:T(8,128)S(1)}, f32[8,32,128,64]{2,3,1,0:T(8,128)}) fusion(f32[8,32,64,128]{3,2,1,0:T(8,128)} %fusion.2, bf16[8,128,32,64]{1,3,2,0:T(8,128)(2,1)} %copy.36, bf16[8,128,32,64]{1,3,2,0:T(8,128)(2,1)} %copy.40, bf16[8,128,32,64]{1,3,2,0:T(8,128)(2,1)} %copy.35, f32[128,128]{1,0:T(8,128)S(1)} %fusion.7), kind=kOutput, calls=%fused_computation.6 | convolution fusion | flops 1088389120 | bytes 29556736 | tf_op jit(solution)/shard_map/nhqk,nkhe->nqhe/dot_general | solution.py:58
  427.0 8.6 %multiply_convert_fusion.1 = bf16[8,128,32,64]{1,3,2,0:T(8,128)(2,1)} fusion(f32[32,64]{1,0:T(8,128)S(1)} %mul.49, f32[8,128,32]{1,2,0:T(8,128)S(1)} %add_rsqrt_fusion, f32[8,32,128,64]{2,3,1,0:T(8,128)} %get-tuple-element.114, f32[8,32,64,128]{3,2,1,0:T(8,128)} %fusion.2), kind=kLoop, calls=%fused_computation.5 | loop fusion | flops 8388608 | bytes 21110784 | tf_op jit(solution)/shard_map/convert_element_type | solution.py:78
  435.6 12.8 %copy.47 = bf16[8,128,32,64]{3,2,1,0:T(8,128)(2,1)} copy(bf16[8,128,32,64]{1,3,2,0:T(8,128)(2,1)} %multiply_convert_fusion.1) | data formatting | bytes 8388608
  448.4 12.3 %reshape.55 = bf16[1024,2048]{1,0:T(8,128)(2,1)} reshape(bf16[8,128,32,64]{3,2,1,0:T(8,128)(2,1)} %copy.47) | data formatting | bytes 8388608
  460.7 79.4 %all-reduce.2.cloned.1.call-done = f32[131072]{0:T(1024)} async-done(((f32[131072]{0:T(1024)}), f32[131072]{0:T(1024)}) %all-reduce.2.cloned.1.call-update) | async-done | bytes 524304 | tf_op jit(solution)/shard_map/psum | solution.py:27
  540.1 1.3 dynamic-slice_multiply_fusion
  (100 shorter events, 104.3 us)
Async XLA Ops:
  7.2 227.2 %all-gather.2.cloned.1.call-start = ((), (), s32[]{:S(2)}) async-start(), calls=%async_computation | async-start | bytes 67633152 | tf_op jit(solution)/shard_map/all_gather | solution.py:14
  55.9 10.8 %copy-start.1 = (f32[2048]{0:T(1024)S(1)}, f32[2048]{0:T(1024)}, u32[]{:S(2)}) copy-start(f32[2048]{0:T(1024)} %param.9) | copy-start | bytes 24580
  66.2 474.0 %all-reduce.2.cloned.1.call-start = ((), (), s32[]{:S(2)}) async-start(), calls=%async_computation.1 | async-start | bytes 1048576 | tf_op jit(solution)/shard_map/psum | solution.py:27
  394.7 12.6 %copy-start = (bf16[8,128,32,64]{1,3,2,0:T(8,128)(2,1)S(1)}, bf16[8,128,32,64]{1,3,2,0:T(8,128)(2,1)}, u32[]{:S(2)}) copy-start(bf16[8,128,32,64]{1,3,2,0:T(8,128)(2,1)} %copy.40) | copy-start | bytes 12582916
Sparse Core Ops, SparseCore 0:
  66.3 168.0 all-gather.1
  394.8 145.2 all-reduce.1
where the time goes:
time: 557 us; the launch traced here: 548 us
  waiting for transfers between devices  206 us (37%)
  other arithmetic  166 us (30%)
  local copies, waits for them, and re-layouts  118 us (21%)
  matrix products  41.3 us (7%)
  between operations  14.1 us (3%)
    select_n x128, other arithmetic, turn(): return jnp.where(reached, new, before)  156 us
    all_gather x1, waiting for transfers between devices, carried_in(): everything = lax.all_gather(array, axis)  127 us
    psum x1, waiting for transfers between devices, from_root(): return lax.psum(jnp.where(mine, array, jnp.zeros_like(array)), axis)  79.4 us
    unnamed x7, local copies, waits for them, and re-layouts  26.1 us
    reshape x2, local copies, waits for them, and re-layouts, shards(): query_grid = queries.reshape(blocks, BLOCK, HEADS, DK)  24.5 us
    reshape x2, local copies, waits for them, and re-layouts, shards(): value_grid = value_rows.reshape(blocks, BLOCK, HEADS, DK)  24.4 us
    reshape x2, local copies, waits for them, and re-layouts, shards(): key_grid = key_rows.reshape(blocks, BLOCK, HEADS, DK)  24.3 us
    dot_general x1, matrix products, shards(): jnp.einsum('nhqk,nkhe->nqhe', weights, value_grid, preferred_element_type...  14.9 us
  transfers between devices with their start and end apart: 2, of which 2 were waited for; matrix products, arithmetic and copies ran while one was open for 20% of the time, Pallas kernels for 0%

commit v1 on v0

--- a/solution.py
+++ b/solution.py
@@ -7,6 +7,11 @@
 HEADS = 32
 DK = 64
 BLOCK = 128
+
+
+def desk_unite(original, ax_name):
+    all_rows = lax.all_gather(original, axis_name=ax_name).sum(axis=0)
+    return all_rows
 
 
 def carried_in(array, axis, combine, identity):
@@ -24,7 +29,7 @@
 
 def from_root(array, axis, root):
     mine = lax.axis_index(axis) == root
-    return lax.psum(jnp.where(mine, array, jnp.zeros_like(array)), axis)
+    return desk_unite(jnp.where(mine, array, jnp.zeros_like(array)), axis)
 
 
 def combine_add(earlier, later):

time: 557 us -> 621 us (1.11)
  other arithmetic: 166 us -> 214 us
  waiting for transfers between devices: 206 us -> 221 us
    psum x1 -> x0, waiting for transfers between devices: 79.4 us -> none  [from_root(): return lax.psum(jnp.where(mine, array, jnp.zeros_like(array)), axis)]
    all_gather x0 -> x1, waiting for transfers between devices: none -> 53.5 us  [desk_unite(): all_rows = lax.all_gather(original, axis_name=ax_name).sum(axis=0)]
    reduce_sum x0 -> x1, other arithmetic: none -> 46.7 us  [desk_unite(): all_rows = lax.all_gather(original, axis_name=ax_name).sum(axis=0)]
    all_gather x1, waiting for transfers between devices: 127 us -> 168 us  [carried_in(): everything = lax.all_gather(array, axis)]
  transfers between devices with their start and end apart: 2 -> 2, of which waited for: 2 -> 2; matrix products, arithmetic and copies ran while one was open for 20% -> 18% of each run, Pallas kernels for 0% -> 0%
where the time goes in v1:
time: 621 us; the launch traced here: 612 us
  waiting for transfers between devices  221 us (36%)
  other arithmetic  214 us (34%)
  local copies, waits for them, and re-layouts  119 us (19%)
  matrix products  41.4 us (7%)
  between operations  14.1 us (2%)
    all_gather x1, waiting for transfers between devices, carried_in(): everything = lax.all_gather(array, axis)  168 us
    select_n x128, other arithmetic, turn(): return jnp.where(reached, new, before)  156 us
    all_gather x1, waiting for transfers between devices, desk_unite(): all_rows = lax.all_gather(original, axis_name=ax_name).sum(axis=0)  53.5 us
    reduce_sum x1, other arithmetic, desk_unite(): all_rows = lax.all_gather(original, axis_name=ax_name).sum(axis=0)  46.7 us
    unnamed x7, local copies, waits for them, and re-layouts  27.2 us
    reshape x2, local copies, waits for them, and re-layouts, shards(): query_grid = queries.reshape(blocks, BLOCK, HEADS, DK)  24.4 us
    reshape x2, local copies, waits for them, and re-layouts, shards(): value_grid = value_rows.reshape(blocks, BLOCK, HEADS, DK)  24.4 us
    reshape x2, local copies, waits for them, and re-layouts, shards(): key_grid = key_rows.reshape(blocks, BLOCK, HEADS, DK)  24.3 us
  transfers between devices with their start and end apart: 2, of which 2 were waited for; matrix products, arithmetic and copies ran while one was open for 18% of the time, Pallas kernels for 0%

profile of v1, /device:TPU:1, one launch (start us, length us, event | category | flops | bytes accessed | tf_op | source)
XLA Modules:
  0.0 612.3 jit_solution(9863920961940308960)
XLA Ops:
  7.2 12.9 %reshape.69 = bf16[8,128,32,64]{3,2,1,0:T(8,128)(2,1)} reshape(bf16[1024,2048]{1,0:T(8,128)(2,1)} %param.7) | data formatting | bytes 8388608 | tf_op jit(solution)/shard_map/reshape | solution.py:43
  20.1 11.5 %copy.35 = bf16[8,128,32,64]{1,3,2,0:T(8,128)(2,1)} copy(bf16[8,128,32,64]{3,2,1,0:T(8,128)(2,1)} %reshape.69) | data formatting | bytes 8388608 | tf_op jit(solution)/shard_map/reshape | solution.py:43
  31.6 12.9 %reshape.70 = bf16[8,128,32,64]{3,2,1,0:T(8,128)(2,1)} reshape(bf16[1024,2048]{1,0:T(8,128)(2,1)} %param.8) | data formatting | bytes 8388608 | tf_op jit(solution)/shard_map/reshape | solution.py:44
  44.4 11.5 %copy.36 = bf16[8,128,32,64]{1,3,2,0:T(8,128)(2,1)} copy(bf16[8,128,32,64]{3,2,1,0:T(8,128)(2,1)} %reshape.70) | data formatting | bytes 8388608 | tf_op jit(solution)/shard_map/reshape | solution.py:44
  55.9 9.0 %fusion.10 = (f32[32,64,64]{2,1,0:T(8,128)S(1)}, f32[8,32,64,64]{3,2,1,0:T(8,128)}) fusion(bf16[8,128,32,64]{1,3,2,0:T(8,128)(2,1)} %copy.35, bf16[8,128,32,64]{1,3,2,0:T(8,128)(2,1)} %copy.36), kind=kOutput, calls=%fused_computation.18 | convolution fusion | flops 269352960 | bytes 13107200 | tf_op jit(solution)/shard_map/nkhd,nkhe->nhde/dot_general | solution.py:45
  66.6 167.7 %all-gather.4.cloned.1.call-done = f32[128,32,4096]{2,1,0:T(8,128)} async-done(((f32[1,32,4096]{2,1,0:T(8,128)}), f32[128,32,4096]{2,1,0:T(8,128)}) %all-gather.4.cloned.1.call-update) | async-done | bytes 67108880 | tf_op jit(solution)/shard_map/all_gather | solution.py:19
  234.3 158.7 %while.14 = (s32[]{:T(128)}, f32[32,4096]{1,0:T(8,128)S(1)}, s32[]{:T(128)}, f32[128,32,4096]{2,1,0:T(8,128)}, s32[]{:T(128)}, /*index=5*/s32[]{:T(128)}) while((s32[]{:T(128)}, f32[32,4096]{1,0:T(8,128)S(1)}, s32[]{:T(128)}, f32[128,32,4096]{2,1,0:T(8,128)}, s32[]{:T(128)}, /*index=5*/s32[]{:T(128)}) %tuple.41), condition=%wide.region_2.3_spmd.clone, body=%wide.region_1.2_spmd.clone.sunk | while | flops 393220 | bytes 1572965 | solution.py:27
  235.5 1.2 add_select_fusion.3
  236.8 1.2 add_select_fusion.3
  238.0 1.2 add_select_fusion.3
  239.3 1.2 add_select_fusion.3
  240.5 1.2 add_select_fusion.3
  241.7 1.2 add_select_fusion.3
  243.0 1.2 add_select_fusion.3
  244.2 1.2 add_select_fusion.3
  245.5 1.2 add_select_fusion.3
  246.7 1.2 add_select_fusion.3
  247.9 1.2 add_select_fusion.3
  249.2 1.2 add_select_fusion.3
  250.4 1.2 add_select_fusion.3
  251.7 1.2 add_select_fusion.3
  252.9 1.2 add_select_fusion.3
  254.1 1.2 add_select_fusion.3
  255.4 1.2 add_select_fusion.3
  256.6 1.2 add_select_fusion.3
  257.9 1.2 add_select_fusion.3
  259.1 1.2 add_select_fusion.3
  260.3 1.2 add_select_fusion.3
  261.6 1.2 add_select_fusion.3
  262.8 1.2 add_select_fusion.3
  264.1 1.2 add_select_fusion.3
  265.3 1.2 add_select_fusion.3
  266.5 1.2 add_select_fusion.3
  267.8 1.2 add_select_fusion.3
  269.0 1.2 add_select_fusion.3
  270.3 1.2 add_select_fusion.3
  271.5 1.2 add_select_fusion.3
  272.7 1.2 add_select_fusion.3
  274.0 1.2 add_select_fusion.3
  275.2 1.2 add_select_fusion.3
  276.5 1.2 add_select_fusion.3
  277.7 1.2 add_select_fusion.3
  278.9 1.2 add_select_fusion.3
  280.2 1.2 add_select_fusion.3
  281.4 1.2 add_select_fusion.3
  282.7 1.2 add_select_fusion.3
  283.9 1.2 add_select_fusion.3
  285.1 1.2 add_select_fusion.3
  286.4 1.2 add_select_fusion.3
  287.6 1.2 add_select_fusion.3
  288.9 1.2 add_select_fusion.3
  393.1 1.4 reshape.64
  394.6 12.9 %reshape.71 = bf16[8,128,32,64]{3,2,1,0:T(8,128)(2,1)} reshape(bf16[1024,2048]{1,0:T(8,128)(2,1)} %param.6) | data formatting | bytes 8388608 | tf_op jit(solution)/shard_map/reshape | solution.py:42
  407.6 11.5 %copy.40 = bf16[8,128,32,64]{1,3,2,0:T(8,128)(2,1)} copy(bf16[8,128,32,64]{3,2,1,0:T(8,128)(2,1)} %reshape.71) | data formatting | bytes 8388608 | tf_op jit(solution)/shard_map/reshape | solution.py:42
  419.1 7.8 %reshape.61 = f32[8,131072]{1,0:T(8,128)} reshape(f32[8,32,64,64]{3,2,1,0:T(8,128)} %get-tuple-element.112) | data formatting | bytes 8388608 | tf_op jit(solution)/shard_map/reshape | solution.py:51
  426.9 8.7 %dot_general.21 = f32[32,64,64,8]{2,1,0,3:T(8,128)} reshape(f32[131072,8]{0,1:T(8,128)} %bitcast.34) | data formatting | bytes 8388608 | tf_op jit(solution)/shard_map/dot_general | solution.py:52
  436.0 13.0 %add_convert_fusion = bf16[8,32,64,64]{3,0,2,1:T(8,128)(2,1)S(1)} fusion(f32[32,64,64]{2,1,0:T(8,128)S(1)} %add.64, f32[32,64,64,8]{2,1,0,3:T(8,128)} %dot_general.21), kind=kOutput, calls=%fused_computation.7 | convolution fusion | flops 102760512 | bytes 6815744 | tf_op jit(solution)/shard_map/dot_general | solution.py:52
  449.0 4.7 fusion.2
  453.7 14.6 %multiply_reduce_fusion = (f32[8,128,32]{1,2,0:T(8,128)S(1)}, f32[8,32,128,64]{2,3,1,0:T(8,128)}) fusion(f32[8,32,64,128]{3,2,1,0:T(8,128)} %fusion.2, bf16[8,128,32,64]{1,3,2,0:T(8,128)(2,1)} %copy.36, bf16[8,128,32,64]{1,3,2,0:T(8,128)(2,1)} %copy.40, bf16[8,128,32,64]{1,3,2,0:T(8,128)(2,1)} %copy.35, f32[128,128]{1,0:T(8,128)S(1)} %fusion.7), kind=kOutput, calls=%fused_computation.6 | convolution fusion | flops 1088389120 | bytes 29556736 | tf_op jit(solution)/shard_map/nhqk,nkhe->nqhe/dot_general | solution.py:63
  468.4 10.5 %multiply_convert_fusion.1 = bf16[8,128,32,64]{1,3,2,0:T(8,128)(2,1)} fusion(f32[32,64]{1,0:T(8,128)S(1)} %mul.49, f32[8,128,32]{1,2,0:T(8,128)S(1)} %add_rsqrt_fusion, f32[8,32,128,64]{2,3,1,0:T(8,128)} %get-tuple-element.114, f32[8,32,64,128]{3,2,1,0:T(8,128)} %fusion.2), kind=kLoop, calls=%fused_computation.5 | loop fusion | flops 8388608 | bytes 21110784 | tf_op jit(solution)/shard_map/convert_element_type | solution.py:83
  478.9 13.1 %copy.47 = bf16[8,128,32,64]{3,2,1,0:T(8,128)(2,1)} copy(bf16[8,128,32,64]{1,3,2,0:T(8,128)(2,1)} %multiply_convert_fusion.1) | data formatting | bytes 8388608
  492.0 12.7 %reshape.68 = bf16[1024,2048]{1,0:T(8,128)(2,1)} reshape(bf16[8,128,32,64]{3,2,1,0:T(8,128)(2,1)} %copy.47) | data formatting | bytes 8388608
  504.7 53.5 %all-gather.6.cloned.1.call-done = f32[128,1,131072]{2,1,0:T(1,128)} async-done(((f32[1,1,131072]{2,1,0:T(1,128)}), f32[128,1,131072]{2,1,0:T(1,128)}) %all-gather.6.cloned.1.call-update) | async-done | bytes 67108880 | tf_op jit(solution)/shard_map/all_gather | solution.py:13
  558.2 46.7 %reduce_sum.29 = f32[131072]{0:T(1024)S(1)} reduce(f32[128,1,131072]{2,1,0:T(1,128)} %all-gather.6.cloned.1.call-done, f32[]{:T(128)} %constant.44.clone.1), dimensions={0,1}, to_apply=%region_4.5 | reduce | flops 16646144 | bytes 67633152 | tf_op jit(solution)/shard_map/reduce_sum | solution.py:13
  (101 shorter events, 105.0 us)
Async XLA Ops:
  7.2 227.1 %all-gather.4.cloned.1.call-start = ((), (), s32[]{:S(2)}) async-start(), calls=%async_computation | async-start | bytes 67633152 | tf_op jit(solution)/shard_map/all_gather | solution.py:19
  65.0 329.6 %copy-start.1 = (f32[2048]{0:T(1024)S(1)}, f32[2048]{0:T(1024)}, u32[]{:S(2)}) copy-start(f32[2048]{0:T(1024)} %param.9) | copy-start | bytes 24580
  66.1 492.1 %all-gather.6.cloned.1.call-start = ((), (), s32[]{:S(2)}) async-start(), calls=%async_computation.1 | async-start | bytes 67633152 | tf_op jit(solution)/shard_map/all_gather | solution.py:13
  436.0 13.0 %copy-start = (bf16[8,128,32,64]{1,3,2,0:T(8,128)(2,1)S(1)}, bf16[8,128,32,64]{1,3,2,0:T(8,128)(2,1)}, u32[]{:S(2)}) copy-start(bf16[8,128,32,64]{1,3,2,0:T(8,128)(2,1)} %copy.40) | copy-start | bytes 12582916
Sparse Core Ops, SparseCore 0:
  66.3 168.0 all-gather.3
  394.7 163.5 all-gather.5
